TPU v7x, 32 devices: a whole 2x2x4 slice. The times are simulated.
32 devices in a mesh: fsdp: 4 (over y, x), ctx: 4 (over z), tp: 2 (over core).
Axes of the slice: x: 2, y: 2, z: 4, core: 2. Of those that a mesh axis runs over, the one named last changes fastest.
Arguments:
- tokens: bfloat16 [8, 1024, 2048], P('fsdp', 'ctx'), may hold values from -6 to 6
- cotangent: bfloat16 [8, 1024, 2048], P('fsdp', 'ctx'), may hold values from -6 to 6
- prefix_len: int32 [8], P('fsdp'), may hold values from 102 to 512
- group_order: int32 [8], replicated, may hold values from 0 to 7, each once
- ln_gain: bfloat16 [2048], replicated, may hold values from 0.25 to 1.75
- ln_bias: bfloat16 [2048], replicated, may hold values from -4 to 4
- query_weight: bfloat16 [2048, 2048], P('fsdp', 'tp'), may hold values from -0.125 to 0.125
- query_bias: bfloat16 [2048], P('tp'), may hold values from -4 to 4
- key_weight: bfloat16 [2048, 2048], P('fsdp', 'tp'), may hold values from -0.125 to 0.125
- key_bias: bfloat16 [2048], P('tp'), may hold values from -4 to 4
- value_weight: bfloat16 [2048, 2048], P('fsdp', 'tp'), may hold values from -0.125 to 0.125
- value_bias: bfloat16 [2048], P('tp'), may hold values from -4 to 4
- out_weight: bfloat16 [2048, 2048], P('fsdp', 'tp'), may hold values from -1 to 1
- out_bias: bfloat16 [2048], replicated, may hold values from -4 to 4
- up_weight: bfloat16 [2048, 8192], P('fsdp', 'tp'), may hold values from -0.125 to 0.125
- up_bias: bfloat16 [8192], P('tp'), may hold values from -4 to 4
- down_weight: bfloat16 [2048, 8192], P('fsdp', 'tp'), may hold values from -0.0625 to 0.0625
- down_bias: bfloat16 [2048], replicated, may hold values from -4 to 4
Outputs:
- output: bfloat16 [8, 1024, 2048], P('fsdp', 'ctx')
- input_grad: bfloat16 [8, 1024, 2048], P('fsdp', 'ctx')
- ln_gain_grad: float32 [2048], replicated
- ln_bias_grad: float32 [2048], replicated
- query_weight_grad: float32 [2048, 2048], P('fsdp', 'tp')
- query_bias_grad: float32 [2048], P('tp')
- key_weight_grad: float32 [2048, 2048], P('fsdp', 'tp')
- key_bias_grad: float32 [2048], P('tp')
- value_weight_grad: float32 [2048, 2048], P('fsdp', 'tp')
- value_bias_grad: float32 [2048], P('tp')
- out_weight_grad: float32 [2048, 2048], P('fsdp', 'tp')
- up_weight_grad: float32 [2048, 8192], P('fsdp', 'tp')
- up_bias_grad: float32 [8192], P('tp')
- down_weight_grad: float32 [2048, 8192], P('fsdp', 'tp')
- out_biases_grad: float32 [2048], replicated
Inputs may be any that keep to these rules, and one draw needn't show every extreme that they name: Each number of 0 to 7 appears once; storage rows k * 128 to k * 128 + 127 of every sequence hold positions group_order[k] * 128 onwards.
All inputs are finite; a program needn't handle non-finite values.
Results may differ from a plain program's by a relative error of at most 0.012.
Values may be sent and summed in bfloat16 or wider, within the bound.
No kernel may reach another device: no remote copies, remote signals or barrier semaphores. Data moves between devices by JAX's collectives and lax.ppermute only.
A program may use at most 448 MiB of HBM per device.

v0:
```python
import jax
import jax.numpy as jnp
from jax import lax
from jax.sharding import PartitionSpec as P

HD = 64
ROT = 32
SEQ_LEN = 1024
masked_fill = -1e30
norm_eps = 1e-05


def positions(group_order, row_start, row_count, group_len):
    row_index = row_start + jnp.arange(row_count, dtype=jnp.int32)
    slot_index = row_index // group_len
    offset = row_index - slot_index * group_len
    matches = slot_index[:, None] == jnp.arange(group_order.shape[0], dtype=jnp.int32)[None, :]
    anchor = jnp.sum(jnp.where(matches, group_order[None, :], 0), axis=1)
    return anchor * group_len + offset


def rotary_tables(places):
    half_rot = ROT // 2
    frequency = jnp.power(10000.0, -2.0 * jnp.arange(half_rot, dtype=jnp.float32) / ROT)
    angles = places.astype(jnp.float32)[:, None] * frequency[None, :]
    return (jnp.cos(angles), jnp.sin(angles))


def rotate(tensor, cosine, sine_vals):
    half_rot = cosine.shape[-1]
    front_part = tensor[..., :half_rot]
    back_part = tensor[..., half_rot : 2 * half_rot]
    rest_part = tensor[..., 2 * half_rot :]
    cosine_rows = cosine[:, None, :]
    sine_rows = sine_vals[:, None, :]
    return jnp.concatenate(
        [
            front_part * cosine_rows - back_part * sine_rows,
            back_part * cosine_rows + front_part * sine_rows,
            rest_part,
        ],
        axis=-1,
    )


def gelu_tanh(values_in):
    return jax.nn.gelu(values_in, approximate=True)


def local(
    tokens,
    cotangent,
    prefix_len,
    group_order,
    ln_gain,
    ln_bias,
    query_weight,
    query_bias,
    key_weight,
    key_bias,
    value_weight,
    value_bias,
    out_weight,
    out_bias,
    up_weight,
    up_bias,
    down_weight,
    down_bias,
):
    seq_count, local_rows, model_width = tokens.shape
    token_count = seq_count * local_rows
    inner_width = query_weight.shape[1]
    local_heads = inner_width // HD
    hidden_units = up_weight.shape[1]
    group_len = SEQ_LEN // group_order.shape[0]
    score_scale = HD ** (-0.5)
    own_place = positions(group_order, lax.axis_index("ctx") * local_rows, local_rows, group_len)
    key_place = positions(group_order, 0, SEQ_LEN, group_len)
    cosine, sine_vals = rotary_tables(own_place)
    allowed = (key_place[None, None, None, :] <= own_place[None, None, :, None]) | (
        key_place[None, None, None, :] < prefix_len[:, None, None, None]
    )
    gathered = (
        lax.all_gather(query_weight, "fsdp", axis=0, tiled=True),
        lax.all_gather(key_weight, "fsdp", axis=0, tiled=True),
        lax.all_gather(value_weight, "fsdp", axis=0, tiled=True),
        lax.all_gather(out_weight, "fsdp", axis=0, tiled=True),
        lax.all_gather(up_weight, "fsdp", axis=0, tiled=True),
        lax.all_gather(down_weight, "fsdp", axis=0, tiled=True),
    )
    w_query, w_key, w_value, w_out, w_up, w_down = gathered
    inputs = tokens.reshape(token_count, model_width).astype(jnp.float32)
    centre = jnp.mean(inputs, axis=-1, keepdims=True)
    centred = inputs - centre
    inv_std = lax.rsqrt(jnp.mean(centred * centred, axis=-1, keepdims=True) + norm_eps)
    normed = centred * inv_std
    norm_gain = ln_gain.astype(jnp.float32)
    hidden = (normed * norm_gain + ln_bias.astype(jnp.float32)).astype(jnp.bfloat16)

    def project(weight, bias_vec):
        return jnp.dot(hidden, weight, preferred_element_type=jnp.float32) + bias_vec.astype(
            jnp.float32
        )

    query_rot = rotate(
        project(w_query, query_bias).reshape(seq_count, local_rows, local_heads, HD),
        cosine,
        sine_vals,
    ).astype(jnp.bfloat16)
    key_rot = (
        rotate(
            project(w_key, key_bias).reshape(seq_count, local_rows, local_heads, HD),
            cosine,
            sine_vals,
        )
        .astype(jnp.bfloat16)
        .reshape(seq_count, local_rows, inner_width)
    )
    value_rows = (
        project(w_value, value_bias)
        .astype(jnp.bfloat16)
        .reshape(seq_count, local_rows, inner_width)
    )
    keys_all, values_all = (
        lax.all_gather(key_rot, "ctx", axis=1, tiled=True),
        lax.all_gather(value_rows, "ctx", axis=1, tiled=True),
    )

    def scores_for(key_block):
        key_heads = key_block.reshape(seq_count, key_block.shape[1], local_heads, HD)
        raw_scores = (
            jnp.einsum("bqhd,bkhd->bhqk", query_rot, key_heads, preferred_element_type=jnp.float32)
            * score_scale
        )
        return jnp.where(allowed, raw_scores, masked_fill)

    masked = scores_for(keys_all)
    row_max = jnp.max(masked, axis=-1, keepdims=True)
    exponent = jnp.exp(masked - row_max)
    row_total = jnp.sum(exponent, axis=-1, keepdims=True)
    attn_probs = (exponent / row_total).astype(jnp.bfloat16)
    log_total = row_max + jnp.log(row_total)
    value_heads = values_all.reshape(seq_count, values_all.shape[1], local_heads, HD)
    context = jnp.einsum(
        "bhqk,bkhd->bqhd", attn_probs, value_heads, preferred_element_type=jnp.float32
    )
    context = context.reshape(token_count, inner_width).astype(jnp.bfloat16)
    up_proj = project(w_up, up_bias)
    activated = gelu_tanh(up_proj).astype(jnp.bfloat16)
    partial_out = jnp.dot(context, w_out.T, preferred_element_type=jnp.float32) + jnp.dot(
        activated, w_down.T, preferred_element_type=jnp.float32
    )
    branches = lax.psum(partial_out, "tp")
    output = inputs + branches + out_bias.astype(jnp.float32) + down_bias.astype(jnp.float32)
    output = output.astype(jnp.bfloat16).reshape(seq_count, local_rows, model_width)
    back_query, back_key, back_value, back_out, back_up, back_down = (
        lax.all_gather(query_weight, "fsdp", axis=0, tiled=True),
        lax.all_gather(key_weight, "fsdp", axis=0, tiled=True),
        lax.all_gather(value_weight, "fsdp", axis=0, tiled=True),
        lax.all_gather(out_weight, "fsdp", axis=0, tiled=True),
        lax.all_gather(up_weight, "fsdp", axis=0, tiled=True),
        lax.all_gather(down_weight, "fsdp", axis=0, tiled=True),
    )
    keys_back, values_back = (
        lax.all_gather(key_rot, "ctx", axis=1, tiled=True),
        lax.all_gather(value_rows, "ctx", axis=1, tiled=True),
    )
    grad_out = cotangent.reshape(token_count, model_width)
    grad_context = jnp.dot(grad_out, back_out, preferred_element_type=jnp.float32).astype(
        jnp.bfloat16
    )
    grad_heads = grad_context.reshape(seq_count, local_rows, local_heads, HD)
    key_heads_back = keys_back.reshape(seq_count, keys_back.shape[1], local_heads, HD)
    value_heads_back = values_back.reshape(seq_count, values_back.shape[1], local_heads, HD)
    probs_back = jnp.exp(scores_for(keys_back) - log_total)
    grad_probs = jnp.einsum(
        "bqhd,bkhd->bhqk", grad_heads, value_heads_back, preferred_element_type=jnp.float32
    )
    row_delta = jnp.sum(probs_back * grad_probs, axis=-1, keepdims=True)
    grad_scores = (probs_back * (grad_probs - row_delta)).astype(jnp.bfloat16)
    probs_low = probs_back.astype(jnp.bfloat16)
    grad_query_rot = (
        jnp.einsum(
            "bhqk,bkhd->bqhd", grad_scores, key_heads_back, preferred_element_type=jnp.float32
        )
        * score_scale
    )
    row_count = local_rows * lax.axis_size("ctx")
    grad_key_part = (
        jnp.einsum("bhqk,bqhd->kbhd", grad_scores, query_rot, preferred_element_type=jnp.float32)
        * score_scale
    )
    grad_value_part = jnp.einsum(
        "bhqk,bqhd->kbhd", probs_low, grad_heads, preferred_element_type=jnp.float32
    )
    key_grads = lax.psum_scatter(
        jnp.concatenate(
            [
                grad_key_part.reshape(row_count, seq_count, inner_width),
                grad_value_part.reshape(row_count, seq_count, inner_width),
            ],
            axis=2,
        ),
        "ctx",
        scatter_dimension=0,
        tiled=True,
    )
    key_grads = jnp.transpose(key_grads, (1, 0, 2))
    key_grad_rot = key_grads[:, :, :inner_width].reshape(seq_count, local_rows, local_heads, HD)
    grad_value = (
        key_grads[:, :, inner_width:].astype(jnp.bfloat16).reshape(token_count, inner_width)
    )
    grad_query = (
        rotate(grad_query_rot, cosine, -sine_vals)
        .astype(jnp.bfloat16)
        .reshape(token_count, inner_width)
    )
    grad_key = (
        rotate(key_grad_rot, cosine, -sine_vals)
        .astype(jnp.bfloat16)
        .reshape(token_count, inner_width)
    )
    grad_activated = jnp.dot(grad_out, back_down, preferred_element_type=jnp.float32)
    gelu_pull = jax.vjp(gelu_tanh, up_proj)[1]
    grad_up = gelu_pull(grad_activated)[0].astype(jnp.bfloat16)
    partial_hidden = (
        jnp.dot(grad_query, back_query.T, preferred_element_type=jnp.float32)
        + jnp.dot(grad_key, back_key.T, preferred_element_type=jnp.float32)
        + jnp.dot(grad_value, back_value.T, preferred_element_type=jnp.float32)
        + jnp.dot(grad_up, back_up.T, preferred_element_type=jnp.float32)
    )
    grad_hidden = lax.psum(partial_hidden, "tp")
    grad_scaled = grad_hidden * norm_gain
    grad_normed = inv_std * (
        grad_scaled
        - jnp.mean(grad_scaled, axis=-1, keepdims=True)
        - normed * jnp.mean(grad_scaled * normed, axis=-1, keepdims=True)
    )
    grad_float = grad_out.astype(jnp.float32)
    input_grad = (
        (grad_float + grad_normed).astype(jnp.bfloat16).reshape(seq_count, local_rows, model_width)
    )
    small_terms = (
        jnp.sum(grad_hidden * normed, axis=0),
        jnp.sum(grad_hidden, axis=0),
        jnp.sum(grad_query, axis=0, dtype=jnp.float32),
        jnp.sum(grad_key, axis=0, dtype=jnp.float32),
        jnp.sum(grad_value, axis=0, dtype=jnp.float32),
        jnp.sum(grad_up, axis=0, dtype=jnp.float32),
        jnp.sum(grad_float, axis=0),
    )
    gain_grad, shift_grad, qbias_grad, kbias_grad, vbias_grad, ubias_grad, obias_grad = lax.psum(
        (
            small_terms[0],
            small_terms[1],
            small_terms[2],
            small_terms[3],
            small_terms[4],
            small_terms[5],
            small_terms[6],
        ),
        ("fsdp", "ctx"),
    )
    grads_in = jnp.concatenate([grad_query, grad_key, grad_value, grad_up], axis=1)
    acts_out = jnp.concatenate([context, activated], axis=1)
    left_part = jnp.einsum("tc,tn->cn", hidden, grads_in, preferred_element_type=jnp.float32)
    right_part = jnp.einsum("tc,tn->cn", grad_out, acts_out, preferred_element_type=jnp.float32)
    scattered = lax.psum_scatter(
        jnp.concatenate([left_part, right_part], axis=1), "fsdp", scatter_dimension=0, tiled=True
    )
    weight_grads = lax.psum(scattered, "ctx")
    edge_two = 2 * inner_width
    edge_three = 3 * inner_width
    edge_four = edge_three + hidden_units
    edge_five = edge_four + inner_width
    return (
        output,
        input_grad,
        gain_grad,
        shift_grad,
        weight_grads[:, :inner_width],
        qbias_grad,
        weight_grads[:, inner_width:edge_two],
        kbias_grad,
        weight_grads[:, edge_two:edge_three],
        vbias_grad,
        weight_grads[:, edge_four:edge_five],
        weight_grads[:, edge_three:edge_four],
        ubias_grad,
        weight_grads[:, edge_five:],
        obias_grad,
    )


def solution(mesh):
    return jax.shard_map(
        local,
        mesh=mesh,
        in_specs=(
            P("fsdp", "ctx", None),
            P("fsdp", "ctx", None),
            P("fsdp"),
            P(),
            P(),
            P(),
            P("fsdp", "tp"),
            P("tp"),
            P("fsdp", "tp"),
            P("tp"),
            P("fsdp", "tp"),
            P("tp"),
            P("fsdp", "tp"),
            P(),
            P("fsdp", "tp"),
            P("tp"),
            P("fsdp", "tp"),
            P(),
        ),
        out_specs=(
            P("fsdp", "ctx", None),
            P("fsdp", "ctx", None),
            P(),
            P(),
            P("fsdp", "tp"),
            P("tp"),
            P("fsdp", "tp"),
            P("tp"),
            P("fsdp", "tp"),
            P("tp"),
            P("fsdp", "tp"),
            P("fsdp", "tp"),
            P("tp"),
            P("fsdp", "tp"),
            P(),
        ),
        check_vma=False,
    )
```

profile of v0, /device:TPU:0, one launch (start us, length us, event | category | flops | bytes accessed | tf_op | source)
XLA Modules:
  0.0 2836.2 jit_solution(8669938643243681293)
XLA Ops:
  14.0 51.3 %all-gather.9.cloned.1.call-done = bf16[2048,1024]{1,0:T(8,128)(2,1)} async-done(((bf16[512,1024]{1,0:T(8,128)(2,1)}), bf16[2048,1024]{1,0:T(8,128)(2,1)}) %all-gather.9.cloned.1.call-update) | async-done | bytes 4194320 | tf_op jit(solution)/shard_map/all_gather | solution.py:86
  65.3 6.1 add_convert_fusion
  72.7 47.3 %all-gather.15.cloned.1.call-done = bf16[2048,1024]{1,0:T(8,128)(2,1)} async-done(((bf16[512,1024]{1,0:T(8,128)(2,1)}), bf16[2048,1024]{1,0:T(8,128)(2,1)}) %all-gather.15.cloned.1.call-update) | async-done | bytes 4194320 | tf_op jit(solution)/shard_map/all_gather | solution.py:85
  119.9 5.8 convolution_add_fusion.1
  125.8 2.9 copy.73
  128.6 3.7 reshape.388
  134.8 39.8 %all-gather.13.cloned.1.call-done = bf16[2048,1024]{1,0:T(8,128)(2,1)} async-done(((bf16[512,1024]{1,0:T(8,128)(2,1)}), bf16[2048,1024]{1,0:T(8,128)(2,1)}) %all-gather.13.cloned.1.call-update) | async-done | bytes 4194320 | tf_op jit(solution)/shard_map/all_gather | solution.py:84
  174.5 5.8 convolution_add_fusion.2
  180.3 4.5 reshape.399
  184.9 8.3 fusion.57
  193.2 3.6 copy.98
  196.8 3.5 copy.97
  210.7 18.2 all-gather.19.cloned.1.call-done
  228.9 5.2 convolution_convert_fusion
  242.1 69.7 %all-gather.11.cloned.1.call-done = bf16[2,1024,1024]{2,1,0:T(8,128)(2,1)} async-done(((bf16[2,256,1024]{2,1,0:T(8,128)(2,1)}), bf16[2,1024,1024]{2,1,0:T(8,128)(2,1)}) %all-gather.11.cloned.1.call-update) | async-done | bytes 4194320 | tf_op jit(solution)/shard_map/all_gather | solution.py:126
  311.7 6.2 copy.68
  318.0 74.9 %all-gather.17.cloned.1.call-done = bf16[2,1024,1024]{1,2,0:T(8,128)(2,1)} async-done(((bf16[2,256,1024]{1,2,0:T(8,128)(2,1)}), bf16[2,1024,1024]{1,2,0:T(8,128)(2,1)}) %all-gather.17.cloned.1.call-update) | async-done | bytes 4194320 | tf_op jit(solution)/shard_map/all_gather | solution.py:125
  392.9 20.1 fusion.59
  412.9 14.6 fusion
  427.5 22.3 multiply_reduce_fusion
  449.8 29.6 %multiply_convert_fusion = bf16[2,16,256,1024]{3,2,1,0:T(8,128)(2,1)} fusion(f32[2,16,256,1024]{3,2,1,0:T(8,128)} %get-tuple-element.72, f32[2,16,256,1024]{3,2,1,0:T(8,128)} %get-tuple-element.70, f32[2,16,256]{2,1,0:T(8,128)S(1)} %get-tuple-element.71, f32[2,16,256]{2,1,0:T(8,128)S(1)} %log_add_fusion), kind=kLoop, calls=%fused_computation.1 | loop fusion | flops 33554432 | bytes 83951616 | tf_op jit(solution)/shard_map/convert_element_type | solution.py:180
  479.4 12.2 broadcast_multiply_fusion
  491.6 17.0 fusion.2
  508.6 11.9 pad_maximum_fusion.1
  521.2 15.1 fusion.43
  539.9 13.7 multiply_bitcast_fusion
  554.9 14.4 fusion.61
  569.3 140.3 %all-gather.23.cloned.1.call-done = bf16[2048,4096]{1,0:T(8,128)(2,1)} async-done(((bf16[512,4096]{1,0:T(8,128)(2,1)}), bf16[2048,4096]{1,0:T(8,128)(2,1)}) %all-gather.23.cloned.1.call-update) | async-done | bytes 16777232 | tf_op jit(solution)/shard_map/all_gather | solution.py:89
  709.6 22.4 convert_reduce_fusion
  732.1 22.1 convolution_bitcast_fusion
  754.2 238.2 %reduce-scatter.3.cloned.1.call-done = f32[256,2,2048]{0,2,1:T(8,128)} async-done(((f32[1024,2,2048]{0,2,1:T(8,128)}), f32[256,2,2048]{0,2,1:T(8,128)}) %reduce-scatter.3.cloned.1.call-update) | async-done | bytes 4194320 | tf_op jit(solution)/shard_map/reduce_scatter | solution.py:196
  992.3 4.0 convert_reduce_fusion.3
  1008.6 26.3 fusion.13
  1034.9 65.5 %pad_maximum_fusion = f32[2048,12288]{1,0:T(8,128)} fusion(f32[2048,5120]{1,0:T(8,128)} %convolution_bitcast_fusion, f32[2048,7168]{1,0:T(8,128)} %fusion.13), kind=kLoop, calls=%fused_computation | loop fusion | flops 25165824 | bytes 201326592 | tf_op jit(solution)/shard_map/concatenate | solution.py:269
  1101.7 6.7 fusion.60
  1108.4 16.2 convolution_add_fusion
  1124.6 4.4 fusion.63
  1129.0 4.4 fusion.62
  1133.4 4.4 fusion.64
  1137.8 18.3 add_add_fusion
  1156.2 773.7 %reduce-scatter.5.cloned.1.call-done = f32[512,12288]{1,0:T(8,128)} async-done(((f32[2048,12288]{1,0:T(8,128)}), f32[512,12288]{1,0:T(8,128)}) %reduce-scatter.5.cloned.1.call-update) | async-done | bytes 25165840 | tf_op jit(solution)/shard_map/reduce_scatter | solution.py:268
  1932.8 39.2 %all-reduce.7.cloned.1.call-done = (f32[512,2048]{1,0:T(8,128)}, f32[512,2048]{1,0:T(8,128)}) async-done(((f32[512,2048]{1,0:T(8,128)}, f32[512,2048]{1,0:T(8,128)}), (f32[512,2048]{1,0:T(8,128)}, f32[512,2048]{1,0:T(8,128)})) %all-reduce.7.cloned.1.call-update) | async-done | bytes 8388624 | tf_op jit(solution)/shard_map/psum | solution.py:153
  1972.0 3.6 fusion.38
  1975.7 82.3 %all-reduce = (f32[2048]{0:T(1024)}, f32[2048]{0:T(1024)}, f32[1024]{0:T(1024)}, f32[1024]{0:T(1024)}, f32[1024]{0:T(1024)}, /*index=5*/f32[4096]{0:T(1024)}, f32[2048]{0:T(1024)}) all-reduce(f32[2048]{0:T(1024)S(1)} %get-tuple-element.15, f32[2048]{0:T(1024)S(1)} %get-tuple-element.18, ...), channel_id=1, replica_groups=mesh['fsdp'=4,'ctx'=4,'tp'=2] {'fsdp','ctx'}, use_global_device_ids=true, to_apply=%region_13.14 | all-reduce | flops 13312 | bytes 106496 | tf_op jit(solution)/shard_map/psum | solution.py:252
  2058.0 6.8 fusion.37
  2064.8 745.8 %all-reduce.5.cloned.1.call-done = f32[512,12288]{1,0:T(8,128)} async-done(((f32[512,12288]{1,0:T(8,128)}), f32[512,12288]{1,0:T(8,128)}) %all-reduce.5.cloned.1.call-update) | async-done | bytes 25165840 | tf_op jit(solution)/shard_map/psum | solution.py:271
  2810.6 7.5 fusion.56
  2818.1 11.1 fusion.55
  (166 shorter events, 50.4 us)
Async XLA Ops:
  7.2 2.9 copy-start
  7.2 4.0 copy-start.34
  7.2 4.0 copy-start.30
  7.2 4.0 copy-start.31
  7.2 58.1 %all-gather.9.cloned.1.call-start = ((), (), s32[]{:S(2)}) async-start(), calls=%async_computation.2 | async-start | bytes 5242880 | tf_op jit(solution)/shard_map/all_gather | solution.py:86
  8.0 112.0 %all-gather.15.cloned.1.call-start = ((), (), s32[]{:S(2)}) async-start(), calls=%async_computation.5 | async-start | bytes 5242880 | tf_op jit(solution)/shard_map/all_gather | solution.py:85
  8.7 165.8 %all-gather.13.cloned.1.call-start = ((), (), s32[]{:S(2)}) async-start(), calls=%async_computation.4 | async-start | bytes 5242880 | tf_op jit(solution)/shard_map/all_gather | solution.py:84
  9.4 219.5 %all-gather.19.cloned.1.call-start = ((), (), s32[]{:S(2)}) async-start(), calls=%async_computation.7 | async-start | bytes 5242880 | tf_op jit(solution)/shard_map/all_gather | solution.py:87
  10.0 301.7 %all-gather.11.cloned.1.call-start = ((), (), s32[]{:S(2)}) async-start(), calls=%async_computation.3 | async-start | bytes 5242880 | tf_op jit(solution)/shard_map/all_gather | solution.py:126
  14.0 57.7 %copy-start.35 = (bf16[1024]{0:T(1024)(128)(2,1)S(1)}, bf16[1024]{0:T(1024)(128)(2,1)}, u32[]{:S(2)}) copy-start(bf16[1024]{0:T(1024)(128)(2,1)} %param.25) | copy-start | bytes 6148
  14.0 57.8 %copy-start.36 = (bf16[1024]{0:T(1024)(128)(2,1)S(1)}, bf16[1024]{0:T(1024)(128)(2,1)}, u32[]{:S(2)}) copy-start(bf16[1024]{0:T(1024)(128)(2,1)} %param.27) | copy-start | bytes 6148
  14.0 57.8 %copy-start.37 = (s32[8]{0:T(128)S(1)}, s32[8]{0:T(128)}, u32[]{:S(2)}) copy-start(s32[8]{0:T(128)} %param.21) | copy-start | bytes 100
  14.0 105.9 %copy-start.3 = (bf16[512,2048]{1,0:T(8,128)(2,1)S(1)}, bf16[512,2048]{1,0:T(8,128)(2,1)}, u32[]{:S(2)}) copy-start(bf16[512,2048]{1,0:T(8,128)(2,1)} %fusion.32) | copy-start | bytes 6291460
  71.5 321.4 %all-gather.17.cloned.1.call-start = ((), (), s32[]{:S(2)}) async-start(), calls=%async_computation.6 | async-start | bytes 5242880 | tf_op jit(solution)/shard_map/all_gather | solution.py:125
  72.7 128.0 %copy-start.16 = (f32[256,16]{0,1:T(8,128)}, f32[256,16]{0,1:T(8,128)S(1)}, u32[]{:S(2)}) copy-start(f32[256,16]{0,1:T(8,128)S(1)} %get-tuple-element.68) | copy-start | bytes 49156
  193.2 7.1 copy-start.5
  200.3 2.0 copy-start.15
  204.9 1.7 copy-start.38
  204.9 350.0 %all-gather.21.cloned.1.call-start = ((), (), s32[]{:S(2)}) async-start(), calls=%async_computation.8 | async-start | bytes 20971520 | tf_op jit(solution)/shard_map/all_gather | solution.py:88
  205.7 503.9 %all-gather.23.cloned.1.call-start = ((), (), s32[]{:S(2)}) async-start(), calls=%async_computation.9 | async-start | bytes 20971520 | tf_op jit(solution)/shard_map/all_gather | solution.py:89
  206.4 785.9 %reduce-scatter.3.cloned.1.call-start = ((), (), s32[]{:S(2)}) async-start(), calls=%async_computation.10 | async-start | bytes 20971520 | tf_op jit(solution)/shard_map/reduce_scatter | solution.py:196
  242.1 150.8 %copy-start.7 = (bf16[2,256,16,32]{1,3,2,0:T(8,128)(2,1)S(1)}, bf16[2,256,16,32]{1,3,2,0:T(8,128)(2,1)}, u32[]{:S(2)}) copy-start(bf16[2,256,16,32]{1,3,2,0:T(8,128)(2,1)} %copy.99) | copy-start | bytes 1572868
  242.1 150.8 %copy-start.8 = (pred[2,256,1024]{2,1,0:T(8,128)(4,1)S(1)}, pred[2,256,1024]{2,1,0:T(8,128)(4,1)}, u32[]{:S(2)}) copy-start(pred[2,256,1024]{2,1,0:T(8,128)(4,1)} %broadcast_or_fusion) | copy-start | bytes 1572868
  242.1 150.8 %copy-start.14 = (bf16[2,256,16,16]{1,3,2,0:T(8,128)(2,1)S(1)}, bf16[2,256,16,16]{1,3,2,0:T(8,128)(2,1)}, u32[]{:S(2)}) copy-start(bf16[2,256,16,16]{1,3,2,0:T(8,128)(2,1)} %get-tuple-element.57) | copy-start | bytes 786436
  412.9 14.6 copy-start.2
  520.5 1409.4 %reduce-scatter.5.cloned.1.call-start = ((), (), s32[]{:S(2)}) async-start(), calls=%async_computation.11 | async-start | bytes 125829120 | tf_op jit(solution)/shard_map/reduce_scatter | solution.py:268
  537.6 1.0 copy-start.9
  539.9 15.0 copy-start.4
  754.1 242.3 %copy-start.17 = (f32[256,16]{0,1:T(8,128)S(1)}, f32[256,16]{0,1:T(8,128)}, u32[]{:S(2)}) copy-start(f32[256,16]{0,1:T(8,128)} %copy-done.16) | copy-start | bytes 49156
  754.1 242.3 %copy-start.20 = (f32[256,16]{0,1:T(8,128)S(1)}, f32[256,16]{0,1:T(8,128)}, u32[]{:S(2)}) copy-start(f32[256,16]{0,1:T(8,128)} %get-tuple-element.66) | copy-start | bytes 49156
  992.3 4.1 copy-start.6
  1000.0 7.1 copy-start.11
  1100.5 1.2 copy-start.10
  1100.5 871.5 %all-reduce.7.cloned.1.call-start = ((), (), s32[]{:S(2)}) async-start(), calls=%async_computation.13 | async-start | bytes 16777216 | tf_op jit(solution)/shard_map/psum | solution.py:153
  1108.4 16.2 copy-start.12
  1108.4 16.2 copy-start.40
  1124.6 4.4 copy-start.13
  1124.6 4.4 copy-start.41
  1129.0 4.4 copy-start.39
  1156.2 1654.4 %all-reduce.5.cloned.1.call-start = ((), (), s32[]{:S(2)}) async-start(), calls=%async_computation.12 | async-start | bytes 50331648 | tf_op jit(solution)/shard_map/psum | solution.py:271
  1929.9 2.7 copy-start.26
  1929.9 2.8 copy-start.25
  1929.9 42.1 %copy-start.1 = (bf16[2,256,2048]{2,1,0:T(8,128)(2,1)S(1)}, bf16[2,256,2048]{2,1,0:T(8,128)(2,1)}, u32[]{:S(2)}) copy-start(bf16[2,256,2048]{2,1,0:T(8,128)(2,1)} %param.18) | copy-start | bytes 6291460
  1929.9 42.1 %copy-start.19 = (f32[2048]{0:T(1024)S(1)}, f32[2048]{0:T(1024)}, u32[]{:S(2)}) copy-start(f32[2048]{0:T(1024)} %copy-done.18) | copy-start | bytes 24580
  1929.9 42.1 %copy-start.22 = (f32[1,2,2,128]{3,1,2,0:T(2,128)S(1)}, f32[1,2,2,128]{3,1,2,0:T(2,128)}, u32[]{:S(2)}) copy-start(f32[1,2,2,128]{3,1,2,0:T(2,128)} %copy-done.21) | copy-start | bytes 6148
  1929.9 42.0 %copy-start.24 = (f32[1,2,2,128]{3,1,2,0:T(2,128)S(1)}, f32[1,2,2,128]{3,1,2,0:T(2,128)}, u32[]{:S(2)}) copy-start(f32[1,2,2,128]{3,1,2,0:T(2,128)} %copy-done.23) | copy-start | bytes 6148
  1930.6 45.0 %copy-start.27 = (f32[4096]{0:T(1024)S(1)}, f32[4096]{0:T(1024)}, u32[]{:S(2)}) copy-start(f32[4096]{0:T(1024)} %get-tuple-element.28) | copy-start | bytes 49156
  1930.6 45.0 %copy-start.28 = (f32[1024]{0:T(1024)S(1)}, f32[1024]{0:T(1024)}, u32[]{:S(2)}) copy-start(f32[1024]{0:T(1024)} %get-tuple-element.30) | copy-start | bytes 12292
  (6 other events, 4.1 us)
Sparse Core Ops, SparseCore 0:
  9.9 55.3 all-gather.8
  67.2 52.6 all-gather.14
  121.8 52.6 all-gather.12
  176.2 52.6 all-gather.18
  230.9 80.7 all-gather.10
  313.7 79.0 all-gather.16
  394.7 155.5 all-gather.20
  552.2 157.4 all-gather.22
  712.0 280.2 reduce-scatter.2
  1100.6 829.2 reduce-scatter.4
  1933.0 38.8 all-reduce.6
  1974.3 836.1 all-reduce.4
where the time goes:
time: 2840 us
  waiting for transfers between devices  2240 us (79%)
  matrix products  263 us (9%)
  other arithmetic  148 us (5%)
  local copies, waits for them, and re-layouts  84.7 us (3%)
  blocking collectives  82.3 us (3%)
    reduce_scatter x1, waiting for transfers between devices, local(): lax.psum_scatter(jnp.concatenate([left_part, right_part], axis=1), 'fsdp'...  774 us
    psum x1, waiting for transfers between devices, local(): weight_grads = lax.psum(scattered, 'ctx')  746 us
    reduce_scatter x1, waiting for transfers between devices, local(): lax.psum_scatter(jnp.concatenate([grad_key_part.reshape(row_count, seq_co...  238 us
    all_gather x1, waiting for transfers between devices, local(): lax.all_gather(down_weight, 'fsdp', axis=0, tiled=True)  140 us
    psum x1, blocking collectives, local(): lax.psum((small_terms[0], small_terms[1], small_terms[2], small_terms[3],...  82.3 us
    all_gather x1, waiting for transfers between devices, local(): lax.all_gather(key_rot, 'ctx', axis=1, tiled=True)  74.9 us
    all_gather x1, waiting for transfers between devices, local(): lax.all_gather(value_rows, 'ctx', axis=1, tiled=True)  69.7 us
    concatenate x1, other arithmetic, local(): jnp.concatenate([left_part, right_part], axis=1)  65.5 us
  transfers between devices with their start and end apart: 12, of which 11 were waited for; matrix products, arithmetic and copies ran while one was open for 13% of the time, Pallas kernels for 0%

commit v1 on v0

--- a/solution.py
+++ b/solution.py
@@ -268,7 +268,8 @@
     scattered = lax.psum_scatter(
         jnp.concatenate([left_part, right_part], axis=1), "fsdp", scatter_dimension=0, tiled=True
     )
-    weight_grads = lax.psum(scattered, "ctx")
+    terms = lax.all_gather(scattered, "ctx", axis=0, tiled=False)
+    weight_grads = terms.sum(axis=0)
     edge_two = 2 * inner_width
     edge_three = 3 * inner_width
     edge_four = edge_three + hidden_units

time: 2840 us -> 3710 us (1.31)
  waiting for transfers between devices: 2240 us -> 2840 us
  blocking collectives: 82.3 us -> 313 us
  other arithmetic: 148 us -> 189 us
    all_gather x0 -> x1, waiting for transfers between devices: none -> 1340 us  [local(): terms = lax.all_gather(scattered, 'ctx', axis=0, tiled=False)]
    psum x1 -> x0, waiting for transfers between devices: 746 us -> none  [local(): weight_grads = lax.psum(scattered, 'ctx')]
    psum x1, blocking collectives: 82.3 us -> 313 us  [local(): lax.psum((small_terms[0], small_terms[1], small_terms[2], small_terms[3],...]
    reduce_sum x0 -> x1, other arithmetic: none -> 40.5 us  [local(): weight_grads = terms.sum(axis=0)]
  transfers between devices with their start and end apart: 12 -> 12, of which waited for: 11 -> 11; matrix products, arithmetic and copies ran while one was open for 13% -> 10% of each run, Pallas kernels for 0% -> 0%
where the time goes in v1:
time: 3710 us; the launch traced here: 3700 us
  waiting for transfers between devices  2840 us (77%)
  blocking collectives  313 us (8%)
  matrix products  263 us (7%)
  other arithmetic  189 us (5%)
  local copies, waits for them, and re-layouts  84.7 us (2%)
    all_gather x1, waiting for transfers between devices, local(): terms = lax.all_gather(scattered, 'ctx', axis=0, tiled=False)  1340 us
    reduce_scatter x1, waiting for transfers between devices, local(): lax.psum_scatter(jnp.concatenate([left_part, right_part], axis=1), 'fsdp'...  774 us
    psum x1, blocking collectives, local(): lax.psum((small_terms[0], small_terms[1], small_terms[2], small_terms[3],...  313 us
    reduce_scatter x1, waiting for transfers between devices, local(): lax.psum_scatter(jnp.concatenate([grad_key_part.reshape(row_count, seq_co...  238 us
    all_gather x1, waiting for transfers between devices, local(): lax.all_gather(down_weight, 'fsdp', axis=0, tiled=True)  140 us
    all_gather x1, waiting for transfers between devices, local(): lax.all_gather(key_rot, 'ctx', axis=1, tiled=True)  74.9 us
  transfers between devices with their start and end apart: 12, of which 11 were waited for; matrix products, arithmetic and copies ran while one was open for 10% of the time, Pallas kernels for 0%

profile of v1, /device:TPU:0, one launch (start us, length us, event | category | flops | bytes accessed | tf_op | source)
XLA Modules:
  0.0 3701.9 jit_solution(15606240173004738463)
XLA Ops:
  14.0 51.3 %all-gather.11.cloned.1.call-done = bf16[2048,1024]{1,0:T(8,128)(2,1)} async-done(((bf16[512,1024]{1,0:T(8,128)(2,1)}), bf16[2048,1024]{1,0:T(8,128)(2,1)}) %all-gather.11.cloned.1.call-update) | async-done | bytes 4194320 | tf_op jit(solution)/shard_map/all_gather | solution.py:86
  65.3 6.1 add_convert_fusion
  72.7 47.2 %all-gather.17.cloned.1.call-done = bf16[2048,1024]{1,0:T(8,128)(2,1)} async-done(((bf16[512,1024]{1,0:T(8,128)(2,1)}), bf16[2048,1024]{1,0:T(8,128)(2,1)}) %all-gather.17.cloned.1.call-update) | async-done | bytes 4194320 | tf_op jit(solution)/shard_map/all_gather | solution.py:85
  119.9 5.8 convolution_add_fusion.1
  128.6 3.7 reshape.388
  134.8 39.8 %all-gather.15.cloned.1.call-done = bf16[2048,1024]{1,0:T(8,128)(2,1)} async-done(((bf16[512,1024]{1,0:T(8,128)(2,1)}), bf16[2048,1024]{1,0:T(8,128)(2,1)}) %all-gather.15.cloned.1.call-update) | async-done | bytes 4194320 | tf_op jit(solution)/shard_map/all_gather | solution.py:84
  174.5 5.8 convolution_add_fusion.2
  180.3 4.5 reshape.400
  184.9 8.3 fusion.57
  193.2 3.6 copy.98
  196.8 3.5 copy.97
  210.7 18.2 all-gather.21.cloned.1.call-done
  228.9 5.1 convolution_convert_fusion
  242.1 69.6 %all-gather.13.cloned.1.call-done = bf16[2,1024,1024]{2,1,0:T(8,128)(2,1)} async-done(((bf16[2,256,1024]{2,1,0:T(8,128)(2,1)}), bf16[2,1024,1024]{2,1,0:T(8,128)(2,1)}) %all-gather.13.cloned.1.call-update) | async-done | bytes 4194320 | tf_op jit(solution)/shard_map/all_gather | solution.py:126
  311.7 6.2 copy.68
  318.0 74.9 %all-gather.19.cloned.1.call-done = bf16[2,1024,1024]{1,2,0:T(8,128)(2,1)} async-done(((bf16[2,256,1024]{1,2,0:T(8,128)(2,1)}), bf16[2,1024,1024]{1,2,0:T(8,128)(2,1)}) %all-gather.19.cloned.1.call-update) | async-done | bytes 4194320 | tf_op jit(solution)/shard_map/all_gather | solution.py:125
  392.9 20.1 fusion.59
  412.9 14.6 fusion
  427.5 22.3 multiply_reduce_fusion
  449.8 29.6 multiply_convert_fusion
  479.4 12.2 broadcast_multiply_fusion
  491.6 17.0 fusion.2
  508.6 11.9 pad_maximum_fusion.1
  521.2 15.1 fusion.43
  539.9 13.7 multiply_bitcast_fusion
  554.9 14.4 fusion.61
  569.3 140.3 %all-gather.25.cloned.1.call-done = bf16[2048,4096]{1,0:T(8,128)(2,1)} async-done(((bf16[512,4096]{1,0:T(8,128)(2,1)}), bf16[2048,4096]{1,0:T(8,128)(2,1)}) %all-gather.25.cloned.1.call-update) | async-done | bytes 16777232 | tf_op jit(solution)/shard_map/all_gather | solution.py:89
  709.6 22.4 convert_reduce_fusion
  732.1 22.1 convolution_bitcast_fusion
  754.2 238.2 %reduce-scatter.3.cloned.1.call-done = f32[256,2,2048]{0,2,1:T(8,128)} async-done(((f32[1024,2,2048]{0,2,1:T(8,128)}), f32[256,2,2048]{0,2,1:T(8,128)}) %reduce-scatter.3.cloned.1.call-update) | async-done | bytes 4194320 | tf_op jit(solution)/shard_map/reduce_scatter | solution.py:196
  992.3 4.0 convert_reduce_fusion.3
  1008.6 26.3 fusion.13
  1034.9 65.5 %pad_maximum_fusion = f32[2048,12288]{1,0:T(8,128)} fusion(f32[2048,5120]{1,0:T(8,128)} %convolution_bitcast_fusion, f32[2048,7168]{1,0:T(8,128)} %fusion.13), kind=kLoop, calls=%fused_computation | loop fusion | flops 25165824 | bytes 201326592 | tf_op jit(solution)/shard_map/concatenate | solution.py:269
  1101.7 6.7 fusion.60
  1108.4 16.2 convolution_add_fusion
  1124.6 4.4 fusion.63
  1129.0 4.4 fusion.62
  1133.4 4.4 fusion.64
  1137.8 18.3 add_add_fusion
  1156.2 773.7 %reduce-scatter.5.cloned.1.call-done = f32[512,12288]{1,0:T(8,128)} async-done(((f32[2048,12288]{1,0:T(8,128)}), f32[512,12288]{1,0:T(8,128)}) %reduce-scatter.5.cloned.1.call-update) | async-done | bytes 25165840 | tf_op jit(solution)/shard_map/reduce_scatter | solution.py:268
  1932.8 39.2 %all-reduce.4.cloned.1.call-done = (f32[512,2048]{1,0:T(8,128)}, f32[512,2048]{1,0:T(8,128)}) async-done(((f32[512,2048]{1,0:T(8,128)}, f32[512,2048]{1,0:T(8,128)}), (f32[512,2048]{1,0:T(8,128)}, f32[512,2048]{1,0:T(8,128)})) %all-reduce.4.cloned.1.call-update) | async-done | bytes 8388624 | tf_op jit(solution)/shard_map/psum | solution.py:153
  1972.0 3.6 fusion.38
  1975.7 312.8 %all-reduce = (f32[2048]{0:T(1024)}, f32[2048]{0:T(1024)}, f32[1024]{0:T(1024)}, f32[1024]{0:T(1024)}, f32[1024]{0:T(1024)}, /*index=5*/f32[4096]{0:T(1024)}, f32[2048]{0:T(1024)}) all-reduce(f32[2048]{0:T(1024)S(1)} %get-tuple-element.15, f32[2048]{0:T(1024)S(1)} %get-tuple-element.18, ...), channel_id=1, replica_groups=mesh['fsdp'=4,'ctx'=4,'tp'=2] {'fsdp','ctx'}, use_global_device_ids=true, to_apply=%region_13.14 | all-reduce | flops 13312 | bytes 106496 | tf_op jit(solution)/shard_map/psum | solution.py:252
  2288.5 6.8 fusion.37
  2295.3 1340.2 %all-gather.27.cloned.1.call-done = f32[2048,12288]{1,0:T(8,128)} async-done(((f32[512,12288]{1,0:T(8,128)}), f32[2048,12288]{1,0:T(8,128)}) %all-gather.27.cloned.1.call-update) | async-done | bytes 100663312 | tf_op jit(solution)/shard_map/all_gather | solution.py:271
  3635.5 40.5 %reduce_sum.158 = f32[512,12288]{1,0:T(8,128)} reduce(f32[4,512,12288]{2,1,0:T(8,128)} %bitcast.18, f32[]{:T(128)} %constant.55.clone.1), dimensions={0}, to_apply=%region_17.18 | reduce | flops 18874368 | bytes 125829120 | tf_op jit(solution)/shard_map/reduce_sum | solution.py:272
  3676.0 7.5 fusion.56
  3683.5 11.1 fusion.55
  (167 shorter events, 53.4 us)
Async XLA Ops:
  7.2 2.9 copy-start
  7.2 4.0 copy-start.34
  7.2 4.0 copy-start.30
  7.2 4.0 copy-start.31
  7.2 58.1 %all-gather.11.cloned.1.call-start = ((), (), s32[]{:S(2)}) async-start(), calls=%async_computation.2 | async-start | bytes 5242880 | tf_op jit(solution)/shard_map/all_gather | solution.py:86
  8.0 112.0 %all-gather.17.cloned.1.call-start = ((), (), s32[]{:S(2)}) async-start(), calls=%async_computation.5 | async-start | bytes 5242880 | tf_op jit(solution)/shard_map/all_gather | solution.py:85
  8.7 165.8 %all-gather.15.cloned.1.call-start = ((), (), s32[]{:S(2)}) async-start(), calls=%async_computation.4 | async-start | bytes 5242880 | tf_op jit(solution)/shard_map/all_gather | solution.py:84
  9.4 219.5 %all-gather.21.cloned.1.call-start = ((), (), s32[]{:S(2)}) async-start(), calls=%async_computation.7 | async-start | bytes 5242880 | tf_op jit(solution)/shard_map/all_gather | solution.py:87
  10.0 301.7 %all-gather.13.cloned.1.call-start = ((), (), s32[]{:S(2)}) async-start(), calls=%async_computation.3 | async-start | bytes 5242880 | tf_op jit(solution)/shard_map/all_gather | solution.py:126
  14.0 57.8 %copy-start.35 = (bf16[1024]{0:T(1024)(128)(2,1)S(1)}, bf16[1024]{0:T(1024)(128)(2,1)}, u32[]{:S(2)}) copy-start(bf16[1024]{0:T(1024)(128)(2,1)} %param.25) | copy-start | bytes 6148
  14.0 57.8 %copy-start.36 = (bf16[1024]{0:T(1024)(128)(2,1)S(1)}, bf16[1024]{0:T(1024)(128)(2,1)}, u32[]{:S(2)}) copy-start(bf16[1024]{0:T(1024)(128)(2,1)} %param.27) | copy-start | bytes 6148
  14.0 57.9 %copy-start.37 = (s32[8]{0:T(128)S(1)}, s32[8]{0:T(128)}, u32[]{:S(2)}) copy-start(s32[8]{0:T(128)} %param.21) | copy-start | bytes 100
  14.0 105.9 %copy-start.3 = (bf16[512,2048]{1,0:T(8,128)(2,1)S(1)}, bf16[512,2048]{1,0:T(8,128)(2,1)}, u32[]{:S(2)}) copy-start(bf16[512,2048]{1,0:T(8,128)(2,1)} %fusion.32) | copy-start | bytes 6291460
  71.5 321.4 %all-gather.19.cloned.1.call-start = ((), (), s32[]{:S(2)}) async-start(), calls=%async_computation.6 | async-start | bytes 5242880 | tf_op jit(solution)/shard_map/all_gather | solution.py:125
  72.7 128.0 %copy-start.16 = (f32[256,16]{0,1:T(8,128)}, f32[256,16]{0,1:T(8,128)S(1)}, u32[]{:S(2)}) copy-start(f32[256,16]{0,1:T(8,128)S(1)} %get-tuple-element.68) | copy-start | bytes 49156
  193.2 7.1 copy-start.5
  200.3 2.0 copy-start.15
  204.9 1.7 copy-start.38
  204.9 350.0 %all-gather.23.cloned.1.call-start = ((), (), s32[]{:S(2)}) async-start(), calls=%async_computation.8 | async-start | bytes 20971520 | tf_op jit(solution)/shard_map/all_gather | solution.py:88
  205.7 503.9 %all-gather.25.cloned.1.call-start = ((), (), s32[]{:S(2)}) async-start(), calls=%async_computation.9 | async-start | bytes 20971520 | tf_op jit(solution)/shard_map/all_gather | solution.py:89
  206.4 785.9 %reduce-scatter.3.cloned.1.call-start = ((), (), s32[]{:S(2)}) async-start(), calls=%async_computation.10 | async-start | bytes 20971520 | tf_op jit(solution)/shard_map/reduce_scatter | solution.py:196
  242.1 150.7 %copy-start.7 = (bf16[2,256,16,32]{1,3,2,0:T(8,128)(2,1)S(1)}, bf16[2,256,16,32]{1,3,2,0:T(8,128)(2,1)}, u32[]{:S(2)}) copy-start(bf16[2,256,16,32]{1,3,2,0:T(8,128)(2,1)} %copy.99) | copy-start | bytes 1572868
  242.1 150.7 %copy-start.8 = (pred[2,256,1024]{2,1,0:T(8,128)(4,1)S(1)}, pred[2,256,1024]{2,1,0:T(8,128)(4,1)}, u32[]{:S(2)}) copy-start(pred[2,256,1024]{2,1,0:T(8,128)(4,1)} %broadcast_or_fusion) | copy-start | bytes 1572868
  242.1 150.7 %copy-start.14 = (bf16[2,256,16,16]{1,3,2,0:T(8,128)(2,1)S(1)}, bf16[2,256,16,16]{1,3,2,0:T(8,128)(2,1)}, u32[]{:S(2)}) copy-start(bf16[2,256,16,16]{1,3,2,0:T(8,128)(2,1)} %get-tuple-element.57) | copy-start | bytes 786436
  412.9 14.6 copy-start.2
  520.5 1409.4 %reduce-scatter.5.cloned.1.call-start = ((), (), s32[]{:S(2)}) async-start(), calls=%async_computation.11 | async-start | bytes 125829120 | tf_op jit(solution)/shard_map/reduce_scatter | solution.py:268
  537.6 1.0 copy-start.9
  539.9 15.0 copy-start.4
  754.1 242.3 %copy-start.17 = (f32[256,16]{0,1:T(8,128)S(1)}, f32[256,16]{0,1:T(8,128)}, u32[]{:S(2)}) copy-start(f32[256,16]{0,1:T(8,128)} %copy-done.16) | copy-start | bytes 49156
  754.1 242.3 %copy-start.20 = (f32[256,16]{0,1:T(8,128)S(1)}, f32[256,16]{0,1:T(8,128)}, u32[]{:S(2)}) copy-start(f32[256,16]{0,1:T(8,128)} %get-tuple-element.66) | copy-start | bytes 49156
  992.3 4.1 copy-start.6
  1000.0 7.1 copy-start.11
  1100.5 1.2 copy-start.10
  1100.5 871.5 %all-reduce.4.cloned.1.call-start = ((), (), s32[]{:S(2)}) async-start(), calls=%async_computation.13 | async-start | bytes 16777216 | tf_op jit(solution)/shard_map/psum | solution.py:153
  1108.4 16.2 copy-start.12
  1108.4 16.2 copy-start.40
  1124.6 4.4 copy-start.13
  1124.6 4.4 copy-start.41
  1129.0 4.4 copy-start.39
  1156.2 2479.4 %all-gather.27.cloned.1.call-start = ((), (), s32[]{:S(2)}) async-start(), calls=%async_computation.12 | async-start | bytes 125829120 | tf_op jit(solution)/shard_map/all_gather | solution.py:271
  1929.9 2.7 copy-start.26
  1929.9 2.8 copy-start.25
  1929.9 42.1 %copy-start.1 = (bf16[2,256,2048]{2,1,0:T(8,128)(2,1)S(1)}, bf16[2,256,2048]{2,1,0:T(8,128)(2,1)}, u32[]{:S(2)}) copy-start(bf16[2,256,2048]{2,1,0:T(8,128)(2,1)} %param.18) | copy-start | bytes 6291460
  1929.9 42.1 %copy-start.19 = (f32[2048]{0:T(1024)S(1)}, f32[2048]{0:T(1024)}, u32[]{:S(2)}) copy-start(f32[2048]{0:T(1024)} %copy-done.18) | copy-start | bytes 24580
  1929.9 42.1 %copy-start.22 = (f32[1,2,2,128]{3,1,2,0:T(2,128)S(1)}, f32[1,2,2,128]{3,1,2,0:T(2,128)}, u32[]{:S(2)}) copy-start(f32[1,2,2,128]{3,1,2,0:T(2,128)} %copy-done.21) | copy-start | bytes 6148
  1929.9 42.0 %copy-start.24 = (f32[1,2,2,128]{3,1,2,0:T(2,128)S(1)}, f32[1,2,2,128]{3,1,2,0:T(2,128)}, u32[]{:S(2)}) copy-start(f32[1,2,2,128]{3,1,2,0:T(2,128)} %copy-done.23) | copy-start | bytes 6148
  1930.6 45.0 %copy-start.27 = (f32[4096]{0:T(1024)S(1)}, f32[4096]{0:T(1024)}, u32[]{:S(2)}) copy-start(f32[4096]{0:T(1024)} %get-tuple-element.28) | copy-start | bytes 49156
  1930.6 45.0 %copy-start.28 = (f32[1024]{0:T(1024)S(1)}, f32[1024]{0:T(1024)}, u32[]{:S(2)}) copy-start(f32[1024]{0:T(1024)} %get-tuple-element.30) | copy-start | bytes 12292
  (6 other events, 4.1 us)
Sparse Core Ops, SparseCore 0:
  9.9 55.3 all-gather.10
  67.2 52.6 all-gather.16
  121.8 52.6 all-gather.14
  176.2 52.6 all-gather.20
  230.9 80.7 all-gather.12
  313.7 79.0 all-gather.18
  394.7 155.5 all-gather.22
  552.2 157.4 all-gather.24
  712.0 280.2 reduce-scatter.2
  1100.6 829.2 reduce-scatter.4
  1933.0 38.8 all-reduce.3
  1973.4 1662.0 all-gather.26
